TPU v7x, 32 devices: a whole 2x2x4 slice. The times are simulated.
32 devices in a mesh: tm: 2 (over core), height: 16 (over z, y, x).
Axes of the slice: x: 2, y: 2, z: 4, core: 2. Of those that a mesh axis runs over, the one named last changes fastest.
Arguments:
- clip: bfloat16 [4, 128, 48, 256], P('tm', 'height'), may hold values from -6 to 6
- teacher: bfloat16 [4, 128, 48, 256], P('tm', 'height'), may hold values from -6 to 6
- kernel_one: bfloat16 [6912, 256], P('height'), may hold values from -0.078125 to 0.078125
- kernel_two: bfloat16 [6912, 256], P('height'), may hold values from -0.078125 to 0.078125
Outputs:
- student: bfloat16 [4, 128, 48, 256], P('tm', 'height')
- grad_one: float32 [6912, 256], P('height')
- grad_two: float32 [6912, 256], P('height')
All inputs are finite; a program needn't handle non-finite values.
Results may differ from a plain program's by a relative error of at most 0.013.
Values may be sent and summed in bfloat16 or wider, within the bound.
No kernel may reach another device: no remote copies, remote signals or barrier semaphores. Data moves between devices by JAX's collectives and lax.ppermute only.
A program may use at most 128 MiB of HBM per device.

v0:
```python
import math
import jax
import jax.numpy as jnp
from jax import lax
from jax.sharding import PartitionSpec as P


def shifted(value, axis, by):
    count = lax.axis_size(axis)
    pairs = [(i, i + by) for i in range(count) if 0 <= i + by < count]
    return lax.ppermute(value, axis, pairs)


def extended_2(cells, sides, width):
    for axis, dim in sides:
        count = lax.axis_size(axis)
        ends = count - 1
        head = lax.slice_in_dim(cells, 0, width, axis=dim)
        tail = lax.slice_in_dim(cells, cells.shape[dim] - width, cells.shape[dim], axis=dim)
        cells = jnp.concatenate(
            [
                lax.ppermute(tail, axis, [(i, (i + 1) % count) for i in range(ends)]),
                cells,
                lax.ppermute(head, axis, [((i + 1) % count, i) for i in range(ends)]),
            ],
            axis=dim,
        )
    return cells


def tap_offsets():
    return [(t_off, h_off, w_off) for t_off in range(3) for h_off in range(3) for w_off in range(3)]


def widen(stacked):
    return jnp.pad(stacked, ((0, 0), (0, 0), (1, 1), (0, 0)))


def clip_edges(rimmed):
    place = lax.axis_index("height")
    blocks = lax.axis_size("height")
    rows_n = rimmed.shape[1]
    row_ids = jnp.arange(rows_n, dtype=jnp.int32)
    cut = jnp.logical_or(
        jnp.logical_and(row_ids == 0, place == 0),
        jnp.logical_and(row_ids == rows_n - 1, place == blocks - 1),
    )
    return jnp.where(cut[None, :, None, None], jnp.zeros_like(rimmed), rimmed)


def causal_patches(values):
    frames_n, height_n, width_n, chans = values.shape
    earlier = shifted(values, "tm", 1)
    extended = jnp.concatenate([earlier, values], axis=0)
    rimmed = clip_edges(extended_2(extended, (("height", 1),), 1))
    padded = widen(rimmed)
    pieces = [
        padded[t_off : t_off + frames_n, h_off : h_off + height_n, w_off : w_off + width_n]
        for t_off, h_off, w_off in tap_offsets()
    ]
    return jnp.stack(pieces, axis=3).reshape(frames_n * height_n * width_n, 27 * chans)


def future_patches(grads):
    frames_n, height_n, width_n, chans = grads.shape
    later = shifted(grads, "tm", -1)
    extended = jnp.concatenate([grads, later], axis=0)
    rimmed = clip_edges(extended_2(extended, (("height", 1),), 1))
    padded = widen(rimmed)
    pieces = [
        padded[
            2 - t_off : 2 - t_off + frames_n,
            2 - h_off : 2 - h_off + height_n,
            2 - w_off : 2 - w_off + width_n,
        ]
        for t_off, h_off, w_off in tap_offsets()
    ]
    return jnp.stack(pieces, axis=3).reshape(frames_n * height_n * width_n, 27, chans)


def reduce_grad(local_grad):
    owned = lax.psum_scatter(
        local_grad.astype(jnp.bfloat16), "height", scatter_dimension=0, tiled=True
    )
    return lax.psum(owned, "tm").astype(jnp.float32)


def shards(clip, teacher, kernel_one, kernel_two):
    frames_n, height_n, width_n, chans = clip.shape
    full_one = lax.all_gather(kernel_one, "height", axis=0, tiled=True)
    patches_clip = causal_patches(clip)
    pre_act = jnp.dot(patches_clip, full_one, preferred_element_type=jnp.float32)
    hidden = jax.nn.silu(pre_act).astype(jnp.bfloat16)
    full_two = lax.all_gather(kernel_two, "height", axis=0, tiled=True)
    patches_hidden = causal_patches(hidden.reshape(frames_n, height_n, width_n, chans))
    branch = jnp.dot(patches_hidden, full_two, preferred_element_type=jnp.float32)
    output = clip.reshape(-1, chans).astype(jnp.float32) + branch
    count_all = frames_n * lax.axis_size("tm") * height_n * lax.axis_size("height") * width_n
    factor = 1.0 / math.sqrt(count_all)
    grad_out = ((output - teacher.reshape(-1, chans).astype(jnp.float32)) * factor).astype(
        jnp.bfloat16
    )
    contract_rows = (((0,), (0,)), ((), ()))
    grad_two = reduce_grad(
        lax.dot_general(patches_hidden, grad_out, contract_rows, preferred_element_type=jnp.float32)
    )
    grad_patches = future_patches(grad_out.reshape(frames_n, height_n, width_n, chans))
    grad_hidden = jnp.einsum(
        "rkc,kdc->rd",
        grad_patches,
        full_two.reshape(27, chans, chans),
        preferred_element_type=jnp.float32,
    )
    sigmoid_pre = jax.nn.sigmoid(pre_act)
    grad_pre = (grad_hidden * sigmoid_pre * (1.0 + pre_act * (1.0 - sigmoid_pre))).astype(
        jnp.bfloat16
    )
    grad_one = reduce_grad(
        lax.dot_general(patches_clip, grad_pre, contract_rows, preferred_element_type=jnp.float32)
    )
    student = output.astype(jnp.bfloat16).reshape(frames_n, height_n, width_n, chans)
    return (student, grad_one, grad_two)


def solution(mesh):
    in_specs = (
        P("tm", "height", None, None),
        P("tm", "height", None, None),
        P("height", None),
        P("height", None),
    )
    out_specs = (P("tm", "height", None, None), P("height", None), P("height", None))
    return jax.shard_map(shards, mesh=mesh, in_specs=in_specs, out_specs=out_specs, check_vma=False)
```

profile of v0, /device:TPU:0, one launch (start us, length us, event | category | flops | bytes accessed | tf_op | source)
XLA Modules:
  0.0 475.6 jit_solution(719828073563204116)
XLA Ops:
  7.9 2.4 collective-permute-start
  10.5 1.4 collective-permute-done
  13.0 4.2 collective-permute-start.1
  17.2 1.3 collective-permute-start.2
  18.5 1.3 collective-permute-done.1
  19.8 4.1 collective-permute-done.2
  26.5 23.9 %copy.7 = bf16[2,8,48,27,256]{4,3,2,1,0:T(8,128)(2,1)S(1)} copy(bf16[2,8,48,27,256]{4,2,1,0,3:T(8,128)(2,1)S(1)} %bitcast_dynamic-update-slice_fusion.18) | data formatting | bytes 21233664 | tf_op jit(solution)/shard_map/stack | solution.py:61
  50.4 10.2 %copy.9 = bf16[96,8,27,256]{3,1,2,0:T(8,128)(2,1)} copy(bf16[96,8,27,256]{3,2,1,0:T(8,128)(2,1)S(1)} %bitcast.205) | data formatting | bytes 21233664
  60.6 23.9 %all-gather.3.cloned.1.call-done = bf16[6912,256]{1,0:T(8,128)(2,1)} async-done(((bf16[432,256]{1,0:T(8,128)(2,1)}), bf16[6912,256]{1,0:T(8,128)(2,1)}) %all-gather.3.cloned.1.call-update) | async-done | bytes 3538960 | tf_op jit(solution)/shard_map/all_gather | solution.py:90
  84.5 8.8 %multiply_convert_fusion = (bf16[768,256]{1,0:T(8,128)(2,1)S(1)}, f32[768,256]{1,0:T(8,128)}) fusion(bf16[768,6912]{1,0:T(8,128)(2,1)} %bitcast.207, bf16[6912,256]{1,0:T(8,128)(2,1)} %all-gather.3.cloned.1.call-done), kind=kOutput, calls=%fused_computation.16 | convolution fusion | flops 2718892032 | bytes 15335424 | tf_op jit(solution)/shard_map/dot_general | solution.py:92
  93.3 1.3 collective-permute-start.3
  94.6 1.3 collective-permute-done.3
  95.9 3.4 collective-permute-start.4
  99.3 1.5 collective-permute-start.5
  101.8 4.1 collective-permute-done.5
  108.6 23.9 %copy.8 = bf16[2,8,48,27,256]{4,3,2,1,0:T(8,128)(2,1)S(1)} copy(bf16[2,8,48,27,256]{4,2,1,0,3:T(8,128)(2,1)S(1)} %bitcast_dynamic-update-slice_fusion) | data formatting | bytes 21233664 | tf_op jit(solution)/shard_map/stack | solution.py:61
  132.5 10.2 %copy.10 = bf16[96,8,27,256]{3,1,2,0:T(8,128)(2,1)} copy(bf16[96,8,27,256]{3,2,1,0:T(8,128)(2,1)S(1)} %bitcast.206) | data formatting | bytes 21233664
  142.7 14.7 %all-gather.5.cloned.1.call-done = bf16[6912,256]{1,0:T(8,128)(2,1)} async-done(((bf16[432,256]{1,0:T(8,128)(2,1)}), bf16[6912,256]{1,0:T(8,128)(2,1)}) %all-gather.5.cloned.1.call-update) | async-done | bytes 3538960 | tf_op jit(solution)/shard_map/all_gather | solution.py:94
  157.4 8.8 %fusion.4 = (bf16[768,256]{1,0:T(8,128)(2,1)S(1)}, bf16[768,256]{1,0:T(8,128)(2,1)}) fusion(bf16[2,8,48,256]{3,2,1,0:T(8,128)(2,1)S(1)} %copy-done.2, bf16[768,6912]{1,0:T(8,128)(2,1)} %bitcast.209, bf16[6912,256]{1,0:T(8,128)(2,1)} %all-gather.5.cloned.1.call-done, bf16[768,256]{1,0:T(8,128)(2,1)S(1)} %bitcast.246), kind=kOutput, calls=%fused_computation.12 | convolution fusion | flops 2719285248 | bytes 15728640 | tf_op jit(solution)/shard_map/dot_general | solution.py:96
  166.2 1.3 collective-permute-start.6
  167.6 4.5 convolution_convert_fusion
  172.2 3.4 collective-permute-start.7
  175.5 1.5 collective-permute-start.8
  177.0 1.5 collective-permute-done.7
  178.5 6.1 %collective-permute-done.8 = bf16[4,1,48,256]{3,2,1,0:T(8,128)(2,1)S(1)} collective-permute-done((bf16[4,1,48,256]{3,2,1,0:T(8,128)(2,1)S(1)}, bf16[4,1,48,256]{3,2,1,0:T(8,128)(2,1)S(1)}, u32[]{:S(2)}, u32[]{:S(2)}) %collective-permute-start.8) | collective-permute-done | bytes 98336 | tf_op jit(solution)/shard_map/ppermute | solution.py:24
  186.6 4.0 pad_slice_fusion
  210.2 20.4 %convolution_convert_fusion.1 = bf16[6912,256]{1,0:T(8,128)(2,1)} fusion(bf16[768,6912]{1,0:T(8,128)(2,1)} %bitcast.208, bf16[768,27,256]{2,0,1:T(8,128)(2,1)} %constant_dynamic-update-slice_fusion.2, bf16[27,256,256]{2,1,0:T(8,128)(2,1)S(1)} %bitcast.247, f32[768,256]{1,0:T(8,128)} %get-tuple-element.41), kind=kOutput, calls=%fused_computation.1 | convolution fusion | flops 5439356928 | bytes 29097984 | tf_op jit(solution)/shard_map/dot_general | solution.py:119
  230.6 75.9 %reduce-scatter.5.cloned.1.call-done = bf16[432,256]{1,0:T(8,128)(2,1)} async-done(((bf16[6912,256]{1,0:T(8,128)(2,1)}), bf16[432,256]{1,0:T(8,128)(2,1)}) %reduce-scatter.5.cloned.1.call-update) | async-done | bytes 221200 | tf_op jit(solution)/shard_map/reduce_scatter | solution.py:82
  306.6 139.2 %reduce-scatter.3.cloned.1.call-done = bf16[432,256]{1,0:T(8,128)(2,1)} async-done(((bf16[6912,256]{1,0:T(8,128)(2,1)}), bf16[432,256]{1,0:T(8,128)(2,1)}) %reduce-scatter.3.cloned.1.call-update) | async-done | bytes 221200 | tf_op jit(solution)/shard_map/reduce_scatter | solution.py:82
  445.8 19.8 %all-reduce.6.cloned.1.call-done = (bf16[432,256]{1,0:T(8,128)(2,1)}, bf16[432,256]{1,0:T(8,128)(2,1)}) async-done(((bf16[432,256]{1,0:T(8,128)(2,1)}, bf16[432,256]{1,0:T(8,128)(2,1)}), (bf16[432,256]{1,0:T(8,128)(2,1)}, bf16[432,256]{1,0:T(8,128)(2,1)})) %all-reduce.6.cloned.1.call-update) | async-done | bytes 442384 | tf_op jit(solution)/shard_map/psum | solution.py:85
  465.6 1.7 convert_element_type.49
  467.3 1.7 convert_element_type.51
  (116 shorter events, 29.7 us)
Async XLA Ops:
  7.2 77.3 %all-gather.3.cloned.1.call-start = ((), (), s32[]{:S(2)}) async-start(), calls=%async_computation.2 | async-start | bytes 3760128 | tf_op jit(solution)/shard_map/all_gather | solution.py:90
  7.9 149.5 %all-gather.5.cloned.1.call-start = ((), (), s32[]{:S(2)}) async-start(), calls=%async_computation.3 | async-start | bytes 3760128 | tf_op jit(solution)/shard_map/all_gather | solution.py:94
  7.9 3.9 collective-permute-start
  10.4 296.2 %reduce-scatter.5.cloned.1.call-start = ((), (), s32[]{:S(2)}) async-start(), calls=%async_computation.5 | async-start | bytes 3760128 | tf_op jit(solution)/shard_map/reduce_scatter | solution.py:82
  13.0 6.8 %collective-permute-start.1 = (bf16[4,1,48,256]{3,2,1,0:T(8,128)(2,1)S(1)}, bf16[4,1,48,256]{3,2,1,0:T(8,128)(2,1)S(1)}, u32[]{:S(2)}, u32[]{:S(2)}) collective-permute-start(bf16[4,1,48,256]{3,2,1,0:T(8,128)(2,1)S(1)} %get-tuple-element.38), channel_id=1, source_target_pairs={{0,1},{1,2},{2,3},{3,4},{4,5},{5,6},{6,7},{7,8},{8,9},{9,10},{10,1... | collective-permute-start | bytes 294920 | tf_op jit(solution)/shard_map/ppermute | solution.py:22
  17.2 6.7 %collective-permute-start.2 = (bf16[4,1,48,256]{3,2,1,0:T(8,128)(2,1)S(1)}, bf16[4,1,48,256]{3,2,1,0:T(8,128)(2,1)S(1)}, u32[]{:S(2)}, u32[]{:S(2)}) collective-permute-start(bf16[4,1,48,256]{3,2,1,0:T(8,128)(2,1)S(1)} %get-tuple-element.39), channel_id=1, source_target_pairs={{1,0},{2,1},{3,2},{4,3},{5,4},{6,5},{7,6},{8,7},{9,8},{10,9},{11,1... | collective-permute-start | bytes 294920 | tf_op jit(solution)/shard_map/ppermute | solution.py:24
  93.3 2.6 collective-permute-start.3
  95.9 5.9 %collective-permute-start.4 = (bf16[4,1,48,256]{3,2,1,0:T(8,128)(2,1)S(1)}, bf16[4,1,48,256]{3,2,1,0:T(8,128)(2,1)S(1)}, u32[]{:S(2)}, u32[]{:S(2)}) collective-permute-start(bf16[4,1,48,256]{3,2,1,0:T(8,128)(2,1)S(1)} %get-tuple-element.36), channel_id=1, source_target_pairs={{0,1},{1,2},{2,3},{3,4},{4,5},{5,6},{6,7},{7,8},{8,9},{9,10},{10,1... | collective-permute-start | bytes 294920 | tf_op jit(solution)/shard_map/ppermute | solution.py:22
  99.3 6.7 %collective-permute-start.5 = (bf16[4,1,48,256]{3,2,1,0:T(8,128)(2,1)S(1)}, bf16[4,1,48,256]{3,2,1,0:T(8,128)(2,1)S(1)}, u32[]{:S(2)}, u32[]{:S(2)}) collective-permute-start(bf16[4,1,48,256]{3,2,1,0:T(8,128)(2,1)S(1)} %get-tuple-element.37), channel_id=1, source_target_pairs={{1,0},{2,1},{3,2},{4,3},{5,4},{6,5},{7,6},{8,7},{9,8},{10,9},{11,1... | collective-permute-start | bytes 294920 | tf_op jit(solution)/shard_map/ppermute | solution.py:24
  132.5 24.9 %copy-start = (bf16[2,8,48,256]{3,2,1,0:T(8,128)(2,1)S(1)}, bf16[2,8,48,256]{3,2,1,0:T(8,128)(2,1)}, u32[]{:S(2)}) copy-start(bf16[2,8,48,256]{3,2,1,0:T(8,128)(2,1)} %param.4) | copy-start | bytes 1179652
  132.5 24.9 %copy-start.2 = (bf16[2,8,48,256]{3,2,1,0:T(8,128)(2,1)S(1)}, bf16[2,8,48,256]{3,2,1,0:T(8,128)(2,1)}, u32[]{:S(2)}) copy-start(bf16[2,8,48,256]{3,2,1,0:T(8,128)(2,1)} %param.5) | copy-start | bytes 1179652
  142.7 24.8 %slice-start = ((s8[10616832]{0:T(1024)(128)(4,1)}), s8[2228224]{0:T(1024)(128)(4,1)S(1)}, s32[]{:S(2)}) async-start(s8[10616832]{0:T(1024)(128)(4,1)} %bitcast.210), calls=%async_computation.7 | async-start | bytes 4456448
  157.4 10.1 %slice-start.1 = ((s8[10616832]{0:T(1024)(128)(4,1)}), s8[4194304]{0:T(1024)(128)(4,1)S(1)}, s32[]{:S(2)}) async-start(s8[10616832]{0:T(1024)(128)(4,1)} %bitcast.210), calls=%async_computation.8 | async-start | bytes 8388608
  157.4 10.1 %slice-start.2 = ((s8[10616832]{0:T(1024)(128)(4,1)}), s8[4194304]{0:T(1024)(128)(4,1)S(1)}, s32[]{:S(2)}) async-start(s8[10616832]{0:T(1024)(128)(4,1)} %bitcast.210), calls=%async_computation.9 | async-start | bytes 8388608
  166.2 5.9 %collective-permute-start.6 = (bf16[2,8,48,256]{3,2,1,0:T(8,128)(2,1)S(1)}, bf16[2,8,48,256]{3,2,1,0:T(8,128)(2,1)S(1)}, u32[]{:S(2)}, u32[]{:S(2)}) collective-permute-start(bf16[2,8,48,256]{3,2,1,0:T(8,128)(2,1)S(1)} %bitcast.232), channel_id=1, source_target_pairs={{16,0},{17,1},{18,2},{19,3},{20,4},{21,5},{22,6},{23,7},{24,8},{25... | collective-permute-start | bytes 1179656 | tf_op jit(solution)/shard_map/ppermute | solution.py:11
  172.1 273.7 %reduce-scatter.3.cloned.1.call-start = ((), (), s32[]{:S(2)}) async-start(), calls=%async_computation.4 | async-start | bytes 3760128 | tf_op jit(solution)/shard_map/reduce_scatter | solution.py:82
  172.2 6.3 %collective-permute-start.7 = (bf16[4,1,48,256]{3,2,1,0:T(8,128)(2,1)S(1)}, bf16[4,1,48,256]{3,2,1,0:T(8,128)(2,1)S(1)}, u32[]{:S(2)}, u32[]{:S(2)}) collective-permute-start(bf16[4,1,48,256]{3,2,1,0:T(8,128)(2,1)S(1)} %get-tuple-element.32), channel_id=1, source_target_pairs={{0,1},{1,2},{2,3},{3,4},{4,5},{5,6},{6,7},{7,8},{8,9},{9,10},{10,1... | collective-permute-start | bytes 294920 | tf_op jit(solution)/shard_map/ppermute | solution.py:22
  175.5 9.0 %collective-permute-start.8 = (bf16[4,1,48,256]{3,2,1,0:T(8,128)(2,1)S(1)}, bf16[4,1,48,256]{3,2,1,0:T(8,128)(2,1)S(1)}, u32[]{:S(2)}, u32[]{:S(2)}) collective-permute-start(bf16[4,1,48,256]{3,2,1,0:T(8,128)(2,1)S(1)} %get-tuple-element.33), channel_id=1, source_target_pairs={{1,0},{2,1},{3,2},{4,3},{5,4},{6,5},{7,6},{8,7},{9,8},{10,9},{11,1... | collective-permute-start | bytes 294920 | tf_op jit(solution)/shard_map/ppermute | solution.py:24
  190.6 19.6 %copy-start.1 = (bf16[6912,256]{1,0:T(8,128)(2,1)S(1)}, bf16[6912,256]{1,0:T(8,128)(2,1)}, u32[]{:S(2)}) copy-start(bf16[6912,256]{1,0:T(8,128)(2,1)} %all-gather.5.cloned.1.call-done) | copy-start | bytes 10616836
  230.6 235.0 %all-reduce.6.cloned.1.call-start = ((), (), s32[]{:S(2)}) async-start(), calls=%async_computation.6 | async-start | bytes 884736 | tf_op jit(solution)/shard_map/psum | solution.py:85
Sparse Core Ops, SparseCore 0:
  10.8 73.6 all-gather.2
  87.3 70.1 all-gather.4
  172.2 134.3 reduce-scatter.4
  311.5 134.1 reduce-scatter.2
  448.0 17.5 all-reduce.5
where the time goes:
time: 476 us
  waiting for transfers between devices  295 us (62%)
  local copies, waits for them, and re-layouts  99.1 us (21%)
  matrix products  42.5 us (9%)
  starting transfers between devices  20.4 us (4%)
  between operations  14.3 us (3%)
    reduce_scatter x2, waiting for transfers between devices, reduce_grad(): lax.psum_scatter(local_grad.astype(jnp.bfloat16), 'height', scatter_dimen...  215 us
    another operation x4, local copies, waits for them, and re-layouts, causal_patches(): jnp.stack(pieces, axis=3).reshape(frames_n * height_n * width_n, 27 * chans)  47.9 us
    unnamed x93, local copies, waits for them, and re-layouts  45.1 us
    all_gather x1, waiting for transfers between devices, shards(): full_one = lax.all_gather(kernel_one, 'height', axis=0, tiled=True)  23.9 us
    dot_general x1, matrix products, shards(): lax.dot_general(patches_clip, grad_pre, contract_rows, preferred_element_...  20.4 us
    psum x1, waiting for transfers between devices, reduce_grad(): return lax.psum(owned, 'tm').astype(jnp.float32)  19.8 us
    all_gather x1, waiting for transfers between devices, shards(): full_two = lax.all_gather(kernel_two, 'height', axis=0, tiled=True)  14.7 us
    ppermute x3, waiting for transfers between devices, extended_2(): lax.ppermute(head, axis, [((i + 1) % count, i) for i in range(ends)])  14.3 us
  transfers between devices with their start and end apart: 14, of which 13 were waited for; matrix products, arithmetic and copies ran while one was open for 28% of the time, Pallas kernels for 0%

commit v1 on v0

--- a/solution.py
+++ b/solution.py
@@ -3,6 +3,23 @@
 import jax.numpy as jnp
 from jax import lax
 from jax.sharding import PartitionSpec as P
+
+
+def hold_tables_on(array_here, dim_k):
+    array_here = jnp.moveaxis(array_here, 0, dim_k)
+    t1 = array_here.shape
+    return array_here.reshape(*t1[:dim_k], t1[dim_k] * t1[dim_k + 1], *t1[dim_k + 2 :])
+
+
+def measure_block(message, peer_axis, in_dim):
+    n_slots = lax.axis_size(peer_axis)
+    shelf = [message]
+    chunks = [(dev, (dev + 1) % n_slots) for dev in range(n_slots)]
+    while len(shelf) < n_slots:
+        shelf.append(lax.ppermute(shelf[-1], peer_axis, perm=chunks))
+    even = lax.axis_index(peer_axis)
+    shelf = jnp.stack(shelf)[(even - jnp.arange(n_slots)) % n_slots]
+    return hold_tables_on(shelf, in_dim)
 
 
 def shifted(value, axis, by):
@@ -87,7 +104,7 @@
 
 def shards(clip, teacher, kernel_one, kernel_two):
     frames_n, height_n, width_n, chans = clip.shape
-    full_one = lax.all_gather(kernel_one, "height", axis=0, tiled=True)
+    full_one = measure_block(kernel_one, "height", 0)
     patches_clip = causal_patches(clip)
     pre_act = jnp.dot(patches_clip, full_one, preferred_element_type=jnp.float32)
     hidden = jax.nn.silu(pre_act).astype(jnp.bfloat16)

time: 476 us -> 573 us (1.20)
  waiting for transfers between devices: 295 us -> 404 us
  local copies, waits for them, and re-layouts: 99.1 us -> 88.6 us
    ppermute x0 -> x15, waiting for transfers between devices: none -> 138 us  [measure_block(): shelf.append(lax.ppermute(shelf[-1], peer_axis, perm=chunks))]
    all_gather x1 -> x0, waiting for transfers between devices: 23.9 us -> none  [shards(): full_one = lax.all_gather(kernel_one, 'height', axis=0, tiled=True)]
    reduce_scatter x2, waiting for transfers between devices: 215 us -> 231 us  [reduce_grad(): lax.psum_scatter(local_grad.astype(jnp.bfloat16), 'height', scatter_dimen...]
    all_gather x1, waiting for transfers between devices: 14.7 us -> 0.01 us  [shards(): full_two = lax.all_gather(kernel_two, 'height', axis=0, tiled=True)]
    unnamed x93 -> x110, local copies, waits for them, and re-layouts: 45.1 us -> 32.6 us
    ppermute x3, starting transfers between devices: 10.9 us -> 4.8 us  [extended_2(): lax.ppermute(tail, axis, [(i, (i + 1) % count) for i in range(ends)])]
  transfers between devices with their start and end apart: 14 -> 28, of which waited for: 13 -> 22; matrix products, arithmetic and copies ran while one was open for 28% -> 21% of each run, Pallas kernels for 0% -> 0%
where the time goes in v1:
time: 573 us; the launch traced here: 572 us
  waiting for transfers between devices  404 us (71%)
  local copies, waits for them, and re-layouts  88.6 us (15%)
  matrix products  42.4 us (7%)
  starting transfers between devices  18.6 us (3%)
  between operations  14.7 us (3%)
    reduce_scatter x2, waiting for transfers between devices, reduce_grad(): lax.psum_scatter(local_grad.astype(jnp.bfloat16), 'height', scatter_dimen...  231 us
    ppermute x15, waiting for transfers between devices, measure_block(): shelf.append(lax.ppermute(shelf[-1], peer_axis, perm=chunks))  138 us
    another operation x4, local copies, waits for them, and re-layouts, causal_patches(): jnp.stack(pieces, axis=3).reshape(frames_n * height_n * width_n, 27 * chans)  47.9 us
    unnamed x110, local copies, waits for them, and re-layouts  32.6 us
    dot_general x1, matrix products, shards(): lax.dot_general(patches_clip, grad_pre, contract_rows, preferred_element_...  20.3 us
    psum x1, waiting for transfers between devices, reduce_grad(): return lax.psum(owned, 'tm').astype(jnp.float32)  19.8 us
  transfers between devices with their start and end apart: 28, of which 22 were waited for; matrix products, arithmetic and copies ran while one was open for 21% of the time, Pallas kernels for 0%

profile of v1, /device:TPU:0, one launch (start us, length us, event | category | flops | bytes accessed | tf_op | source)
XLA Modules:
  0.0 572.4 jit_solution(14651005296974437553)
XLA Ops:
  7.2 3.2 collective-permute-start
  10.4 2.3 collective-permute-start.3
  13.8 7.5 %collective-permute-done.3 = bf16[432,256]{1,0:T(8,128)(2,1)} collective-permute-done((bf16[432,256]{1,0:T(8,128)(2,1)}, bf16[432,256]{1,0:T(8,128)(2,1)}, u32[]{:S(2)}, u32[]{:S(2)}) %collective-permute-start.3) | collective-permute-done | bytes 221216 | tf_op jit(solution)/shard_map/ppermute | solution.py:19
  27.7 6.9 %collective-permute-done.4 = bf16[432,256]{1,0:T(8,128)(2,1)S(1)} collective-permute-done((bf16[432,256]{1,0:T(8,128)(2,1)}, bf16[432,256]{1,0:T(8,128)(2,1)S(1)}, u32[]{:S(2)}, u32[]{:S(2)}) %collective-permute-start.4) | collective-permute-done | bytes 221216 | tf_op jit(solution)/shard_map/ppermute | solution.py:19
  37.3 23.9 %copy.7 = bf16[2,8,48,27,256]{4,3,2,1,0:T(8,128)(2,1)S(1)} copy(bf16[2,8,48,27,256]{4,2,1,0,3:T(8,128)(2,1)S(1)} %bitcast_dynamic-update-slice_fusion.18) | data formatting | bytes 21233664 | tf_op jit(solution)/shard_map/stack | solution.py:78
  61.2 10.2 %copy.9 = bf16[96,8,27,256]{3,1,2,0:T(8,128)(2,1)} copy(bf16[96,8,27,256]{3,2,1,0:T(8,128)(2,1)S(1)} %bitcast.240) | data formatting | bytes 21233664
  72.7 14.2 %collective-permute-done.6 = bf16[432,256]{1,0:T(8,128)(2,1)S(1)} collective-permute-done((bf16[432,256]{1,0:T(8,128)(2,1)S(1)}, bf16[432,256]{1,0:T(8,128)(2,1)S(1)}, u32[]{:S(2)}, u32[]{:S(2)}) %collective-permute-start.6) | collective-permute-done | bytes 221216 | tf_op jit(solution)/shard_map/ppermute | solution.py:19
  86.9 9.5 %collective-permute-done.7 = bf16[432,256]{1,0:T(8,128)(2,1)S(1)} collective-permute-done((bf16[432,256]{1,0:T(8,128)(2,1)S(1)}, bf16[432,256]{1,0:T(8,128)(2,1)S(1)}, u32[]{:S(2)}, u32[]{:S(2)}) %collective-permute-start.7) | collective-permute-done | bytes 221216 | tf_op jit(solution)/shard_map/ppermute | solution.py:19
  96.5 9.5 %collective-permute-done.8 = bf16[432,256]{1,0:T(8,128)(2,1)S(1)} collective-permute-done((bf16[432,256]{1,0:T(8,128)(2,1)S(1)}, bf16[432,256]{1,0:T(8,128)(2,1)S(1)}, u32[]{:S(2)}, u32[]{:S(2)}) %collective-permute-start.8) | collective-permute-done | bytes 221216 | tf_op jit(solution)/shard_map/ppermute | solution.py:19
  106.0 9.5 %collective-permute-done.9 = bf16[432,256]{1,0:T(8,128)(2,1)S(1)} collective-permute-done((bf16[432,256]{1,0:T(8,128)(2,1)S(1)}, bf16[432,256]{1,0:T(8,128)(2,1)S(1)}, u32[]{:S(2)}, u32[]{:S(2)}) %collective-permute-start.9) | collective-permute-done | bytes 221216 | tf_op jit(solution)/shard_map/ppermute | solution.py:19
  115.5 10.3 %collective-permute-done.10 = bf16[432,256]{1,0:T(8,128)(2,1)S(1)} collective-permute-done((bf16[432,256]{1,0:T(8,128)(2,1)S(1)}, bf16[432,256]{1,0:T(8,128)(2,1)S(1)}, u32[]{:S(2)}, u32[]{:S(2)}) %collective-permute-start.10) | collective-permute-done | bytes 221216 | tf_op jit(solution)/shard_map/ppermute | solution.py:19
  125.8 11.4 %collective-permute-done.11 = bf16[432,256]{1,0:T(8,128)(2,1)S(1)} collective-permute-done((bf16[432,256]{1,0:T(8,128)(2,1)S(1)}, bf16[432,256]{1,0:T(8,128)(2,1)S(1)}, u32[]{:S(2)}, u32[]{:S(2)}) %collective-permute-start.11) | collective-permute-done | bytes 221216 | tf_op jit(solution)/shard_map/ppermute | solution.py:19
  137.2 11.2 %collective-permute-done.12 = bf16[432,256]{1,0:T(8,128)(2,1)S(1)} collective-permute-done((bf16[432,256]{1,0:T(8,128)(2,1)S(1)}, bf16[432,256]{1,0:T(8,128)(2,1)S(1)}, u32[]{:S(2)}, u32[]{:S(2)}) %collective-permute-start.12) | collective-permute-done | bytes 221216 | tf_op jit(solution)/shard_map/ppermute | solution.py:19
  148.5 10.3 %collective-permute-done.13 = bf16[432,256]{1,0:T(8,128)(2,1)S(1)} collective-permute-done((bf16[432,256]{1,0:T(8,128)(2,1)S(1)}, bf16[432,256]{1,0:T(8,128)(2,1)S(1)}, u32[]{:S(2)}, u32[]{:S(2)}) %collective-permute-start.13) | collective-permute-done | bytes 221216 | tf_op jit(solution)/shard_map/ppermute | solution.py:19
  158.8 9.5 %collective-permute-done.14 = bf16[432,256]{1,0:T(8,128)(2,1)S(1)} collective-permute-done((bf16[432,256]{1,0:T(8,128)(2,1)S(1)}, bf16[432,256]{1,0:T(8,128)(2,1)S(1)}, u32[]{:S(2)}, u32[]{:S(2)}) %collective-permute-start.14) | collective-permute-done | bytes 221216 | tf_op jit(solution)/shard_map/ppermute | solution.py:19
  168.3 9.5 %collective-permute-done.15 = bf16[432,256]{1,0:T(8,128)(2,1)S(1)} collective-permute-done((bf16[432,256]{1,0:T(8,128)(2,1)S(1)}, bf16[432,256]{1,0:T(8,128)(2,1)S(1)}, u32[]{:S(2)}, u32[]{:S(2)}) %collective-permute-start.15) | collective-permute-done | bytes 221216 | tf_op jit(solution)/shard_map/ppermute | solution.py:19
  177.9 9.5 %collective-permute-done.16 = bf16[432,256]{1,0:T(8,128)(2,1)S(1)} collective-permute-done((bf16[432,256]{1,0:T(8,128)(2,1)S(1)}, bf16[432,256]{1,0:T(8,128)(2,1)S(1)}, u32[]{:S(2)}, u32[]{:S(2)}) %collective-permute-start.16) | collective-permute-done | bytes 221216 | tf_op jit(solution)/shard_map/ppermute | solution.py:19
  187.4 9.5 %collective-permute-done.17 = bf16[432,256]{1,0:T(8,128)(2,1)S(1)} collective-permute-done((bf16[432,256]{1,0:T(8,128)(2,1)S(1)}, bf16[432,256]{1,0:T(8,128)(2,1)S(1)}, u32[]{:S(2)}, u32[]{:S(2)}) %collective-permute-start.17) | collective-permute-done | bytes 221216 | tf_op jit(solution)/shard_map/ppermute | solution.py:19
  196.9 2.6 gather_fusion
  199.5 8.8 %multiply_convert_fusion = (bf16[768,256]{1,0:T(8,128)(2,1)S(1)}, f32[768,256]{1,0:T(8,128)}) fusion(bf16[768,6912]{1,0:T(8,128)(2,1)} %bitcast.242, bf16[6912,256]{1,0:T(8,128)(2,1)} %bitcast.248), kind=kOutput, calls=%fused_computation.17 | convolution fusion | flops 2718892032 | bytes 15335424 | tf_op jit(solution)/shard_map/dot_general | solution.py:109
  215.2 4.1 collective-permute-done.20
  222.0 23.9 %copy.8 = bf16[2,8,48,27,256]{4,3,2,1,0:T(8,128)(2,1)S(1)} copy(bf16[2,8,48,27,256]{4,2,1,0,3:T(8,128)(2,1)S(1)} %bitcast_dynamic-update-slice_fusion) | data formatting | bytes 21233664 | tf_op jit(solution)/shard_map/stack | solution.py:78
  245.9 10.2 %copy.10 = bf16[96,8,27,256]{3,1,2,0:T(8,128)(2,1)} copy(bf16[96,8,27,256]{3,2,1,0:T(8,128)(2,1)S(1)} %bitcast.241) | data formatting | bytes 21233664
  256.1 8.8 %fusion.4 = (bf16[768,256]{1,0:T(8,128)(2,1)S(1)}, bf16[768,256]{1,0:T(8,128)(2,1)}) fusion(bf16[2,8,48,256]{3,2,1,0:T(8,128)(2,1)S(1)} %copy-done.3, bf16[768,6912]{1,0:T(8,128)(2,1)} %bitcast.244, bf16[6912,256]{1,0:T(8,128)(2,1)} %all-gather.2.cloned.1.call-done, bf16[768,256]{1,0:T(8,128)(2,1)S(1)} %bitcast.282), kind=kOutput, calls=%fused_computation.13 | convolution fusion | flops 2719285248 | bytes 15728640 | tf_op jit(solution)/shard_map/dot_general | solution.py:113
  266.3 4.5 convolution_convert_fusion
  275.2 6.1 %collective-permute-done.23 = bf16[4,1,48,256]{3,2,1,0:T(8,128)(2,1)S(1)} collective-permute-done((bf16[4,1,48,256]{3,2,1,0:T(8,128)(2,1)S(1)}, bf16[4,1,48,256]{3,2,1,0:T(8,128)(2,1)S(1)}, u32[]{:S(2)}, u32[]{:S(2)}) %collective-permute-start.23) | collective-permute-done | bytes 98336 | tf_op jit(solution)/shard_map/ppermute | solution.py:41
  281.9 4.1 pad_slice_fusion
  286.9 3.9 copy-done.1
  290.8 20.3 %convolution_convert_fusion.1 = bf16[6912,256]{1,0:T(8,128)(2,1)} fusion(bf16[768,6912]{1,0:T(8,128)(2,1)} %bitcast.243, bf16[768,27,256]{2,0,1:T(8,128)(2,1)} %copy-done.1, bf16[27,256,256]{2,1,0:T(8,128)(2,1)S(1)} %bitcast.283, f32[768,256]{1,0:T(8,128)} %get-tuple-element.41), kind=kOutput, calls=%fused_computation.2 | convolution fusion | flops 5439356928 | bytes 29097984 | tf_op jit(solution)/shard_map/dot_general | solution.py:136
  311.1 91.9 %reduce-scatter.5.cloned.1.call-done = bf16[432,256]{1,0:T(8,128)(2,1)} async-done(((bf16[6912,256]{1,0:T(8,128)(2,1)}), bf16[432,256]{1,0:T(8,128)(2,1)}) %reduce-scatter.5.cloned.1.call-update) | async-done | bytes 221200 | tf_op jit(solution)/shard_map/reduce_scatter | solution.py:99
  403.0 139.5 %reduce-scatter.3.cloned.1.call-done = bf16[432,256]{1,0:T(8,128)(2,1)} async-done(((bf16[6912,256]{1,0:T(8,128)(2,1)}), bf16[432,256]{1,0:T(8,128)(2,1)}) %reduce-scatter.3.cloned.1.call-update) | async-done | bytes 221200 | tf_op jit(solution)/shard_map/reduce_scatter | solution.py:99
  542.6 19.8 %all-reduce.6.cloned.1.call-done = (bf16[432,256]{1,0:T(8,128)(2,1)}, bf16[432,256]{1,0:T(8,128)(2,1)}) async-done(((bf16[432,256]{1,0:T(8,128)(2,1)}, bf16[432,256]{1,0:T(8,128)(2,1)}), (bf16[432,256]{1,0:T(8,128)(2,1)}, bf16[432,256]{1,0:T(8,128)(2,1)})) %all-reduce.6.cloned.1.call-update) | async-done | bytes 442384 | tf_op jit(solution)/shard_map/psum | solution.py:102
  (164 shorter events, 31.2 us)
Async XLA Ops:
  7.2 249.0 %all-gather.2.cloned.1.call-start = ((), (), s32[]{:S(2)}) async-start(), calls=%async_computation.2 | async-start | bytes 3760128 | tf_op jit(solution)/shard_map/all_gather | solution.py:111
  7.2 15.1 %collective-permute-start = (bf16[2,8,48,256]{3,2,1,0:T(8,128)(2,1)}, bf16[2,8,48,256]{3,2,1,0:T(8,128)(2,1)}, u32[]{:S(2)}, u32[]{:S(2)}) collective-permute-start(bf16[2,8,48,256]{3,2,1,0:T(8,128)(2,1)} %param.4), channel_id=1, source_target_pairs={{0,16},{1,17},{2,18},{3,19},{4,20},{5,21},{6,22},{7,23},{8,24},{9,... | collective-permute-start | bytes 1179656 | tf_op jit(solution)/shard_map/ppermute | solution.py:28
  10.4 10.9 %collective-permute-start.3 = (bf16[432,256]{1,0:T(8,128)(2,1)}, bf16[432,256]{1,0:T(8,128)(2,1)}, u32[]{:S(2)}, u32[]{:S(2)}) collective-permute-start(bf16[432,256]{1,0:T(8,128)(2,1)} %param.6), channel_id=1, source_target_pairs={{0,1},{1,2},{2,3},{3,4},{4,5},{5,6},{6,7},{7,8},{8,9},{9,10},{10,1... | collective-permute-start | bytes 663560 | tf_op jit(solution)/shard_map/ppermute | solution.py:19
  12.7 390.3 %reduce-scatter.5.cloned.1.call-start = ((), (), s32[]{:S(2)}) async-start(), calls=%async_computation.4 | async-start | bytes 3760128 | tf_op jit(solution)/shard_map/reduce_scatter | solution.py:99
  21.3 13.4 %collective-permute-start.4 = (bf16[432,256]{1,0:T(8,128)(2,1)}, bf16[432,256]{1,0:T(8,128)(2,1)S(1)}, u32[]{:S(2)}, u32[]{:S(2)}) collective-permute-start(bf16[432,256]{1,0:T(8,128)(2,1)} %collective-permute-done.3), channel_id=1, source_target_pairs={{0,1},{1,2},{2,3},{3,4},{4,5},{5,6},{6,7},{7,8},{8,9},{9,10},{10,1... | collective-permute-start | bytes 663560 | tf_op jit(solution)/shard_map/ppermute | solution.py:19
  24.4 10.3 %collective-permute-start.1 = (bf16[4,1,48,256]{3,2,1,0:T(8,128)(2,1)S(1)}, bf16[4,1,48,256]{3,2,1,0:T(8,128)(2,1)S(1)}, u32[]{:S(2)}, u32[]{:S(2)}) collective-permute-start(bf16[4,1,48,256]{3,2,1,0:T(8,128)(2,1)S(1)} %get-tuple-element.38), channel_id=1, source_target_pairs={{0,1},{1,2},{2,3},{3,4},{4,5},{5,6},{6,7},{7,8},{8,9},{9,10},{10,1... | collective-permute-start | bytes 294920 | tf_op jit(solution)/shard_map/ppermute | solution.py:39
  26.4 8.3 %collective-permute-start.2 = (bf16[4,1,48,256]{3,2,1,0:T(8,128)(2,1)S(1)}, bf16[4,1,48,256]{3,2,1,0:T(8,128)(2,1)S(1)}, u32[]{:S(2)}, u32[]{:S(2)}) collective-permute-start(bf16[4,1,48,256]{3,2,1,0:T(8,128)(2,1)S(1)} %get-tuple-element.39), channel_id=1, source_target_pairs={{1,0},{2,1},{3,2},{4,3},{5,4},{6,5},{7,6},{8,7},{9,8},{10,9},{11,1... | collective-permute-start | bytes 294920 | tf_op jit(solution)/shard_map/ppermute | solution.py:41
  34.7 36.7 %collective-permute-start.5 = (bf16[432,256]{1,0:T(8,128)(2,1)S(1)}, bf16[432,256]{1,0:T(8,128)(2,1)S(1)}, u32[]{:S(2)}, u32[]{:S(2)}) collective-permute-start(bf16[432,256]{1,0:T(8,128)(2,1)S(1)} %collective-permute-done.4), channel_id=1, source_target_pairs={{0,1},{1,2},{2,3},{3,4},{4,5},{5,6},{6,7},{7,8},{8,9},{9,10},{10,1... | collective-permute-start | bytes 663560 | tf_op jit(solution)/shard_map/ppermute | solution.py:19
  71.4 15.5 %collective-permute-start.6 = (bf16[432,256]{1,0:T(8,128)(2,1)S(1)}, bf16[432,256]{1,0:T(8,128)(2,1)S(1)}, u32[]{:S(2)}, u32[]{:S(2)}) collective-permute-start(bf16[432,256]{1,0:T(8,128)(2,1)S(1)} %collective-permute-done.5), channel_id=1, source_target_pairs={{0,1},{1,2},{2,3},{3,4},{4,5},{5,6},{6,7},{7,8},{8,9},{9,10},{10,1... | collective-permute-start | bytes 663560 | tf_op jit(solution)/shard_map/ppermute | solution.py:19
  86.9 9.5 %collective-permute-start.7 = (bf16[432,256]{1,0:T(8,128)(2,1)S(1)}, bf16[432,256]{1,0:T(8,128)(2,1)S(1)}, u32[]{:S(2)}, u32[]{:S(2)}) collective-permute-start(bf16[432,256]{1,0:T(8,128)(2,1)S(1)} %collective-permute-done.6), channel_id=1, source_target_pairs={{0,1},{1,2},{2,3},{3,4},{4,5},{5,6},{6,7},{7,8},{8,9},{9,10},{10,1... | collective-permute-start | bytes 663560 | tf_op jit(solution)/shard_map/ppermute | solution.py:19
  96.4 9.5 %collective-permute-start.8 = (bf16[432,256]{1,0:T(8,128)(2,1)S(1)}, bf16[432,256]{1,0:T(8,128)(2,1)S(1)}, u32[]{:S(2)}, u32[]{:S(2)}) collective-permute-start(bf16[432,256]{1,0:T(8,128)(2,1)S(1)} %collective-permute-done.7), channel_id=1, source_target_pairs={{0,1},{1,2},{2,3},{3,4},{4,5},{5,6},{6,7},{7,8},{8,9},{9,10},{10,1... | collective-permute-start | bytes 663560 | tf_op jit(solution)/shard_map/ppermute | solution.py:19
  106.0 9.5 %collective-permute-start.9 = (bf16[432,256]{1,0:T(8,128)(2,1)S(1)}, bf16[432,256]{1,0:T(8,128)(2,1)S(1)}, u32[]{:S(2)}, u32[]{:S(2)}) collective-permute-start(bf16[432,256]{1,0:T(8,128)(2,1)S(1)} %collective-permute-done.8), channel_id=1, source_target_pairs={{0,1},{1,2},{2,3},{3,4},{4,5},{5,6},{6,7},{7,8},{8,9},{9,10},{10,1... | collective-permute-start | bytes 663560 | tf_op jit(solution)/shard_map/ppermute | solution.py:19
  115.5 10.3 %collective-permute-start.10 = (bf16[432,256]{1,0:T(8,128)(2,1)S(1)}, bf16[432,256]{1,0:T(8,128)(2,1)S(1)}, u32[]{:S(2)}, u32[]{:S(2)}) collective-permute-start(bf16[432,256]{1,0:T(8,128)(2,1)S(1)} %collective-permute-done.9), channel_id=1, source_target_pairs={{0,1},{1,2},{2,3},{3,4},{4,5},{5,6},{6,7},{7,8},{8,9},{9,10},{10,1... | collective-permute-start | bytes 663560 | tf_op jit(solution)/shard_map/ppermute | solution.py:19
  125.8 11.4 %collective-permute-start.11 = (bf16[432,256]{1,0:T(8,128)(2,1)S(1)}, bf16[432,256]{1,0:T(8,128)(2,1)S(1)}, u32[]{:S(2)}, u32[]{:S(2)}) collective-permute-start(bf16[432,256]{1,0:T(8,128)(2,1)S(1)} %collective-permute-done.10), channel_id=1, source_target_pairs={{0,1},{1,2},{2,3},{3,4},{4,5},{5,6},{6,7},{7,8},{8,9},{9,10},{10,1... | collective-permute-start | bytes 663560 | tf_op jit(solution)/shard_map/ppermute | solution.py:19
  137.2 11.2 %collective-permute-start.12 = (bf16[432,256]{1,0:T(8,128)(2,1)S(1)}, bf16[432,256]{1,0:T(8,128)(2,1)S(1)}, u32[]{:S(2)}, u32[]{:S(2)}) collective-permute-start(bf16[432,256]{1,0:T(8,128)(2,1)S(1)} %collective-permute-done.11), channel_id=1, source_target_pairs={{0,1},{1,2},{2,3},{3,4},{4,5},{5,6},{6,7},{7,8},{8,9},{9,10},{10,1... | collective-permute-start | bytes 663560 | tf_op jit(solution)/shard_map/ppermute | solution.py:19
  148.4 10.4 %collective-permute-start.13 = (bf16[432,256]{1,0:T(8,128)(2,1)S(1)}, bf16[432,256]{1,0:T(8,128)(2,1)S(1)}, u32[]{:S(2)}, u32[]{:S(2)}) collective-permute-start(bf16[432,256]{1,0:T(8,128)(2,1)S(1)} %collective-permute-done.12), channel_id=1, source_target_pairs={{0,1},{1,2},{2,3},{3,4},{4,5},{5,6},{6,7},{7,8},{8,9},{9,10},{10,1... | collective-permute-start | bytes 663560 | tf_op jit(solution)/shard_map/ppermute | solution.py:19
  158.8 9.5 %collective-permute-start.14 = (bf16[432,256]{1,0:T(8,128)(2,1)S(1)}, bf16[432,256]{1,0:T(8,128)(2,1)S(1)}, u32[]{:S(2)}, u32[]{:S(2)}) collective-permute-start(bf16[432,256]{1,0:T(8,128)(2,1)S(1)} %collective-permute-done.13), channel_id=1, source_target_pairs={{0,1},{1,2},{2,3},{3,4},{4,5},{5,6},{6,7},{7,8},{8,9},{9,10},{10,1... | collective-permute-start | bytes 663560 | tf_op jit(solution)/shard_map/ppermute | solution.py:19
  168.3 9.5 %collective-permute-start.15 = (bf16[432,256]{1,0:T(8,128)(2,1)S(1)}, bf16[432,256]{1,0:T(8,128)(2,1)S(1)}, u32[]{:S(2)}, u32[]{:S(2)}) collective-permute-start(bf16[432,256]{1,0:T(8,128)(2,1)S(1)} %collective-permute-done.14), channel_id=1, source_target_pairs={{0,1},{1,2},{2,3},{3,4},{4,5},{5,6},{6,7},{7,8},{8,9},{9,10},{10,1... | collective-permute-start | bytes 663560 | tf_op jit(solution)/shard_map/ppermute | solution.py:19
  177.8 9.5 %collective-permute-start.16 = (bf16[432,256]{1,0:T(8,128)(2,1)S(1)}, bf16[432,256]{1,0:T(8,128)(2,1)S(1)}, u32[]{:S(2)}, u32[]{:S(2)}) collective-permute-start(bf16[432,256]{1,0:T(8,128)(2,1)S(1)} %collective-permute-done.15), channel_id=1, source_target_pairs={{0,1},{1,2},{2,3},{3,4},{4,5},{5,6},{6,7},{7,8},{8,9},{9,10},{10,1... | collective-permute-start | bytes 663560 | tf_op jit(solution)/shard_map/ppermute | solution.py:19
  187.4 9.5 %collective-permute-start.17 = (bf16[432,256]{1,0:T(8,128)(2,1)S(1)}, bf16[432,256]{1,0:T(8,128)(2,1)S(1)}, u32[]{:S(2)}, u32[]{:S(2)}) collective-permute-start(bf16[432,256]{1,0:T(8,128)(2,1)S(1)} %collective-permute-done.16), channel_id=1, source_target_pairs={{0,1},{1,2},{2,3},{3,4},{4,5},{5,6},{6,7},{7,8},{8,9},{9,10},{10,1... | collective-permute-start | bytes 663560 | tf_op jit(solution)/shard_map/ppermute | solution.py:19
  208.4 2.6 collective-permute-start.18
  211.0 4.2 collective-permute-start.19
  212.3 7.0 %collective-permute-start.20 = (bf16[4,1,48,256]{3,2,1,0:T(8,128)(2,1)S(1)}, bf16[4,1,48,256]{3,2,1,0:T(8,128)(2,1)S(1)}, u32[]{:S(2)}, u32[]{:S(2)}) collective-permute-start(bf16[4,1,48,256]{3,2,1,0:T(8,128)(2,1)S(1)} %get-tuple-element.37), channel_id=1, source_target_pairs={{1,0},{2,1},{3,2},{4,3},{5,4},{6,5},{7,6},{8,7},{9,8},{10,9},{11,1... | collective-permute-start | bytes 294920 | tf_op jit(solution)/shard_map/ppermute | solution.py:41
  245.8 10.3 %copy-start = (bf16[2,8,48,256]{3,2,1,0:T(8,128)(2,1)S(1)}, bf16[2,8,48,256]{3,2,1,0:T(8,128)(2,1)}, u32[]{:S(2)}) copy-start(bf16[2,8,48,256]{3,2,1,0:T(8,128)(2,1)} %param.4) | copy-start | bytes 1179652
  245.9 10.3 %copy-start.3 = (bf16[2,8,48,256]{3,2,1,0:T(8,128)(2,1)S(1)}, bf16[2,8,48,256]{3,2,1,0:T(8,128)(2,1)}, u32[]{:S(2)}) copy-start(bf16[2,8,48,256]{3,2,1,0:T(8,128)(2,1)} %param.5) | copy-start | bytes 1179652
  256.1 10.1 %slice-start = ((s8[10616832]{0:T(1024)(128)(4,1)}), s8[2228224]{0:T(1024)(128)(4,1)S(1)}, s32[]{:S(2)}) async-start(s8[10616832]{0:T(1024)(128)(4,1)} %bitcast.245), calls=%async_computation.6 | async-start | bytes 4456448
  256.1 10.1 %slice-start.1 = ((s8[10616832]{0:T(1024)(128)(4,1)}), s8[4194304]{0:T(1024)(128)(4,1)S(1)}, s32[]{:S(2)}) async-start(s8[10616832]{0:T(1024)(128)(4,1)} %bitcast.245), calls=%async_computation.7 | async-start | bytes 8388608
  265.0 5.9 %collective-permute-start.21 = (bf16[2,8,48,256]{3,2,1,0:T(8,128)(2,1)S(1)}, bf16[2,8,48,256]{3,2,1,0:T(8,128)(2,1)S(1)}, u32[]{:S(2)}, u32[]{:S(2)}) collective-permute-start(bf16[2,8,48,256]{3,2,1,0:T(8,128)(2,1)S(1)} %bitcast.268), channel_id=1, source_target_pairs={{16,0},{17,1},{18,2},{19,3},{20,4},{21,5},{22,6},{23,7},{24,8},{25... | collective-permute-start | bytes 1179656 | tf_op jit(solution)/shard_map/ppermute | solution.py:28
  270.8 271.8 %reduce-scatter.3.cloned.1.call-start = ((), (), s32[]{:S(2)}) async-start(), calls=%async_computation.3 | async-start | bytes 3760128 | tf_op jit(solution)/shard_map/reduce_scatter | solution.py:99
  270.9 4.3 collective-permute-start.22
  272.3 9.0 %collective-permute-start.23 = (bf16[4,1,48,256]{3,2,1,0:T(8,128)(2,1)S(1)}, bf16[4,1,48,256]{3,2,1,0:T(8,128)(2,1)S(1)}, u32[]{:S(2)}, u32[]{:S(2)}) collective-permute-start(bf16[4,1,48,256]{3,2,1,0:T(8,128)(2,1)S(1)} %get-tuple-element.33), channel_id=1, source_target_pairs={{1,0},{2,1},{3,2},{4,3},{5,4},{6,5},{7,6},{8,7},{9,8},{10,9},{11,1... | collective-permute-start | bytes 294920 | tf_op jit(solution)/shard_map/ppermute | solution.py:41
  311.1 251.3 %all-reduce.6.cloned.1.call-start = ((), (), s32[]{:S(2)}) async-start(), calls=%async_computation.5 | async-start | bytes 884736 | tf_op jit(solution)/shard_map/psum | solution.py:102
  (3 other events, 18.9 us)
Sparse Core Ops, SparseCore 0:
  12.8 75.3 all-gather.1
  270.9 132.0 reduce-scatter.4
  408.1 134.3 reduce-scatter.2
  544.8 17.5 all-reduce.5
